TPU v7x, 32 devices: a whole 2x2x4 slice. The times are simulated.
32 devices in a mesh: col: 8 (over y, x, core), row: 4 (over z).
Axes of the slice: x: 2, y: 2, z: 4, core: 2. Of those that a mesh axis runs over, the one named last changes fastest.
Arguments:
- rhs: bfloat16 [6, 8, 4, 128, 512], P(None, 'col', 'row'), may hold values from -6 to 6
- diag_inv: bfloat16 [6, 8, 4, 128, 128], P(None, 'col', 'row'), may hold values from -0.5 to 0.5
- factor: bfloat16 [5, 8, 4, 8, 2, 128, 128], P(None, 'col', 'row'), may hold values from -0.1875 to 0.1875
- columns: int32 [5, 8, 4, 8, 2], P(None, 'col', 'row'), may hold values from 0 to 3, as said below
Outputs:
- solution: bfloat16 [6, 8, 4, 128, 512], P(None, 'col', 'row')
Inputs may be any that keep to these rules, and one draw needn't show every extreme that they name: The 2 entries of columns for one factor row block and one column owner are distinct.
All inputs are finite; a program needn't handle non-finite values.
Results may differ from a plain program's by a relative error of at most 0.025.
Values may be sent and summed in bfloat16 or wider, within the bound.
A program may use at most 128 MiB of HBM per device.

v0:
```python
import functools

import jax
import jax.numpy as jnp
from jax import lax
from jax.experimental import pallas as pl
from jax.experimental.pallas import tpu as pltpu
from jax.sharding import PartitionSpec as P

MESH = pl.DeviceIdType.MESH
CHUNKS = 2
AHEAD = 1
REACH = (-2, 2, -1, 1)


def kernel(n_col, n_row, rhs, diag, fac, cols, cols_hbm, out, *scratch):
    steps, rows, width = rhs.shape[0], rhs.shape[3], rhs.shape[4]
    slots = fac.shape[4]
    chips = n_col // 2
    half = width // 2
    wide = half // CHUNKS
    fold = max(1, 128 // wide)
    tall = rows // fold
    links = steps - 1

    (rv, dv, fv, cp, own, sent, landed, stage,
     in_loc, in_send, in_recv, z_send, z_recv, c_send, c_recv,
     o_loc, o_send, o_recv) = scratch[:18]
    panels = scratch[18:]

    col = lax.axis_index("col")
    row = lax.axis_index("row")
    core = lax.rem(col, 2)
    chip = lax.div(col, 2)
    partner = col + 1 - 2 * core
    mine = pl.ds(pl.multiple_of(core * half, half), half)
    theirs = pl.ds(pl.multiple_of((1 - core) * half, half), half)

    def to(c, r):
        return {"col": c, "row": r}

    def spans(total):
        return [pl.ds(0, 1), pl.ds(1, total - 1)]

    local = {}
    for g in range(2):
        a, b = spans(steps)[g], spans(links)[g]
        local["rhs", g] = pltpu.make_async_copy(rhs.at[a, 0, 0, :, mine], rv.at[a, 0], in_loc.at[0, g])
        local["diag", g] = pltpu.make_async_copy(diag.at[a, 0, 0], dv.at[a, 0], in_loc.at[1, g])
        local["fac", g] = pltpu.make_async_copy(fac.at[b, 0, 0], fv.at[b, 0], in_loc.at[2, g])
    for c in local.values():
        c.start()

    barrier = pltpu.get_barrier_semaphore()
    pl.semaphore_signal(barrier, inc=1, device_id=to(partner, row), device_id_type=MESH)
    count = chips
    for step in REACH:
        near = (row + step >= 0) & (row + step < n_row)
        count = count + near.astype(jnp.int32)

        @pl.when(near)
        def _():
            pl.semaphore_signal(barrier, inc=1, device_id=to(col, row + step), device_id_type=MESH)

    for d in range(1, chips):
        other = lax.rem(chip + d, chips) * 2 + core
        pl.semaphore_signal(barrier, inc=1, device_id=to(other, row), device_id_type=MESH)
    pl.semaphore_wait(barrier, count)

    def remote(src, dst, send, recv, device):
        return pltpu.make_async_remote_copy(
            src_ref=src, dst_ref=dst, send_sem=send, recv_sem=recv,
            device_id=device, device_id_type=MESH)

    pair = to(partner, row)
    cross = {}
    for g in range(2):
        a, b = spans(steps)[g], spans(links)[g]
        cross["rhs", g] = remote(rhs.at[a, 0, 0, :, theirs], rv.at[a, 1], in_send.at[0, g], in_recv.at[0, g], pair)
        cross["diag", g] = remote(diag.at[a, 0, 0], dv.at[a, 1], in_send.at[1, g], in_recv.at[1, g], pair)
        cross["fac", g] = remote(fac.at[b, 0, 0], fv.at[b, 1], in_send.at[2, g], in_recv.at[2, g], pair)
        if g == 0:
            cross["cols", g] = remote(cols_hbm, cp, in_send.at[3, g], in_recv.at[3, g], pair)
    for c in cross.values():
        c.start()

    def arrived(name, g):
        if (name, g) in local:
            local[name, g].wait()
        cross[name, g].wait_recv()

    def pack(x):
        return x if fold == 1 else jnp.concatenate(
            [x[i * tall:(i + 1) * tall] for i in range(fold)], axis=1)

    def unpack(x):
        return x if fold == 1 else jnp.concatenate(
            [x[:, i * wide:(i + 1) * wide] for i in range(fold)], axis=0)

    def part(ch):
        return pl.ds(ch * wide, wide)

    def z_copy(s, ch, source, step):
        buf = panels[s * CHUNKS + ch]
        way = REACH.index(step)
        return remote(buf.at[source], buf.at[source], z_send.at[s, ch, way, source],
                      z_recv.at[s, ch, source], to(col, row + step))

    def reaches(step):
        return (row + step >= 0) & (row + step < n_row)

    def z_own(s, ch):
        for step in REACH:
            @pl.when(reaches(step))
            def _():
                z_copy(s, ch, row, step).start()

    def hop(s, ch, h):
        if h >= n_row:
            return
        for _ in (0,):
            for step in (-1, 1):
                @pl.when(reaches(-step * h))
                def _():
                    z_copy(s, ch, row - step * h, step).wait_recv()
                    if 2 <= h < n_row - 1:
                        @pl.when(reaches(step))
                        def _():
                            z_copy(s, ch, row - step * h, step).start()

    def z_sent(s, ch):
        for _ in (0,):
            for step in REACH:
                @pl.when(reaches(step))
                def _():
                    z_copy(s, ch, row, step).wait_send()
            for h in range(2, n_row - 1):
                for step in (-1, 1):
                    @pl.when(reaches(step) & reaches(-step * h))
                    def _():
                        z_copy(s, ch, row - step * h, step).wait_send()

    def c_copy(s, ch, d):
        other = lax.rem(chip + d, chips) * 2 + core
        return remote(sent.at[s, ch, d - 1], landed.at[s, ch, d - 1], c_send.at[s, ch, d - 1],
                      c_recv.at[s, ch, d - 1], to(other, row))

    def out_copies(s, ch):
        first, size = (ch + 1 - fold) * wide, fold * wide
        span = pl.ds(pl.multiple_of(core * half + first, size), size)
        src = stage.at[s, :, :, pl.ds(first, size)]
        keep = pltpu.make_async_copy(src.at[0], out.at[s, 0, 0, :, span], o_loc.at[s, ch])
        give = remote(src.at[1], out.at[s, 0, 0, :, span], o_send.at[s, ch], o_recv.at[s, ch], pair)
        return keep, give

    def solve(s, ch):
        if s > 0:
            for d in range(1, chips):
                c_copy(s - 1, ch, d).wait_recv()
        for k in range(2):
            block = dv[s, k]
            right = rv[s, k, :, part(ch)]
            if s == 0:
                x = jnp.dot(block, right, preferred_element_type=jnp.float32)
            else:
                total = own[ch, k]
                for d in range(1, chips):
                    total = total + unpack(landed[s - 1, ch, d - 1, k]).astype(jnp.float32)
                rem = right.astype(jnp.float32) - total
                high = rem.astype(jnp.bfloat16)
                low = (rem - high.astype(jnp.float32)).astype(jnp.bfloat16)
                x = jnp.dot(jnp.concatenate([block, block], axis=1),
                            jnp.concatenate([high, low], axis=0),
                            preferred_element_type=jnp.float32)
            x = x.astype(jnp.bfloat16)
            if s < links:
                panels[s * CHUNKS + ch][row, k] = pack(x)
            stage[s, k, :, part(ch)] = x
        if s < links:
            z_own(s, ch)
        if ch % fold == fold - 1:
            for c in out_copies(s, ch):
                c.start()

    def term(s, ch, other, k):
        buf = panels[s * CHUNKS + ch]
        t = other * 2 + (core if k == 0 else 1 - core)
        left, right = [], []
        for slot, index in ((0, cols), (1, cp)):
            for m in range(slots):
                left.append(fv[s, slot, t, m])
                right.append(unpack(buf[index[s, 0, 0, m, t], slot]))
        return jnp.dot(jnp.concatenate(left, axis=1), jnp.concatenate(right, axis=0),
                       preferred_element_type=jnp.float32)

    def spread(s, ch):
        def one(d):
            other = lax.rem(chip + d, chips)
            for k in range(2):
                sent[s, ch, d - 1, k] = pack(term(s, ch, other, k).astype(jnp.bfloat16))
            c_copy(s, ch, d).start()

        if chips <= 4:
            for d in range(1, chips):
                one(d)
        else:
            @pl.loop(1, chips)
            def _(d):
                one(d)
        for k in range(2):
            own[ch, k] = term(s, ch, chip, k)

    def ready(s, names):
        if s < 2:
            for name in names:
                arrived(name, s)

    for s in range(steps):
        ready(s, ("rhs", "diag"))
        for ch in range(CHUNKS):
            solve(s, ch)
        if s < links:
            ready(s, ("fac", "cols") if s == 0 else ("fac",))
            for ch in range(AHEAD):
                hop(s, ch, 2)
            for ch in range(CHUNKS):
                if ch + AHEAD < CHUNKS:
                    hop(s, ch + AHEAD, 2)
                for h in range(3, n_row):
                    hop(s, ch, h)
                hop(s, ch, 1)
                spread(s, ch)

    for c in cross.values():
        c.wait_send()
    for s in range(steps):
        for ch in range(CHUNKS):
            if ch % fold == fold - 1:
                keep, give = out_copies(s, ch)
                keep.wait()
                give.wait()
            if s < links:
                z_sent(s, ch)
                for d in range(1, chips):
                    c_copy(s, ch, d).wait_send()


def on_device(n_col, n_row, rhs, diag_inv, factor, columns):
    steps, rows, width = rhs.shape[0], rhs.shape[3], rhs.shape[4]
    columns = jnp.swapaxes(columns, 3, 4)
    targets, slots = factor.shape[3], factor.shape[4]
    chips, half = n_col // 2, width // 2
    wide, links = half // CHUNKS, steps - 1
    fold = max(1, 128 // wide)
    packed = (rows // fold, wide * fold)
    bf16 = jnp.bfloat16
    dma = pltpu.SemaphoreType.DMA
    scratch = [
        pltpu.VMEM((steps, 2, rows, half), bf16),
        pltpu.VMEM((steps, 2, rows, rows), bf16),
        pltpu.VMEM((links, 2, targets, slots, rows, rows), bf16),
        pltpu.SMEM(columns.shape, jnp.int32),
        pltpu.VMEM((CHUNKS, 2, rows, wide), jnp.float32),
        pltpu.VMEM((links, CHUNKS, chips - 1, 2) + packed, bf16),
        pltpu.VMEM((links, CHUNKS, chips - 1, 2) + packed, bf16),
        pltpu.VMEM((steps, 2, rows, half), bf16),
        dma((3, 2)), dma((4, 2)), dma((4, 2)),
        dma((links, CHUNKS, len(REACH), n_row)), dma((links, CHUNKS, n_row)),
        dma((links, CHUNKS, chips - 1)), dma((links, CHUNKS, chips - 1)),
        dma((steps, CHUNKS)), dma((steps, CHUNKS)), dma((steps, CHUNKS)),
    ] + [pltpu.VMEM((n_row, 2) + packed, bf16) for _ in range(links * CHUNKS)]
    anywhere = pl.BlockSpec(memory_space=pl.ANY)
    return pl.pallas_call(
        functools.partial(kernel, n_col, n_row),
        out_shape=jax.ShapeDtypeStruct(rhs.shape, bf16),
        in_specs=[anywhere, anywhere, anywhere, pl.BlockSpec(memory_space=pltpu.SMEM), anywhere],
        out_specs=anywhere,
        scratch_shapes=scratch,
        compiler_params=pltpu.CompilerParams(
            collective_id=0, has_side_effects=True, vmem_limit_bytes=60 * 1024 * 1024),
        name="levels",
    )(rhs, diag_inv, factor, columns, columns)


def solution(mesh):
    n_col, n_row = mesh.shape["col"], mesh.shape["row"]
    return jax.shard_map(
        functools.partial(on_device, n_col, n_row),
        mesh=mesh,
        in_specs=(
            P(None, "col", "row", None, None),
            P(None, "col", "row", None, None),
            P(None, "col", "row", None, None, None, None),
            P(None, "col", "row", None, None),
        ),
        out_specs=P(None, "col", "row", None, None),
        check_vma=False,
    )
```

profile of v0, /device:TPU:0, one launch (start us, length us, event | category | flops | bytes accessed | tf_op | source)
XLA Modules:
  0.0 81.5 jit_solution(17173323946170289285)
XLA Ops:
  0.0 79.4 %levels.1 = bf16[6,1,1,128,512]{4,3,2,1,0:T(8,128)(2,1)} custom-call(bf16[6,1,1,128,512]{4,3,2,1,0:T(8,128)(2,1)} %rhs.1, bf16[6,1,1,128,128]{4,3,2,1,0:T(8,128)(2,1)} %diag.1, bf16[5,1,1,8,2,128,128]{6,5,4,3,2,1,0:T(8,128)(2,1)} %fac.1, s32[5,1,1,2,8]{4,3,2,1,0:T(2,128)} %bitcast.1, s32[5,1,1,2,8]{4,3,2,1,0:T(2,128)} %bitcast.2), custom_call_target="tpu_custom_call" | custom-call | tf_op jit(solution)/shard_map/levels/pallas_call | solution.py:273
  79.4 2.1 %copy.6 = bf16[6,1,1,128,512]{4,3,2,1,0:T(8,128)(2,1)} copy(bf16[6,1,1,128,512]{4,3,2,1,0:T(8,128)(2,1)} %levels.1) | data formatting | bytes 1572864
where the time goes:
time: 81.6 us; the launch traced here: 81.5 us
  Pallas kernels  79.4 us (97%)
  local copies, waits for them, and re-layouts  2.1 us (3%)
    pallas_call x1, Pallas kernels, on_device(): pl.pallas_call(functools.partial(kernel, n_col, n_row), out_shape=jax.Sha...  79.4 us
    unnamed x1, local copies, waits for them, and re-layouts  2.1 us

commit v1 on v0

v1 whole, which is shorter than its diff:
```python
import functools

import jax
import jax.numpy as jnp
from jax import lax
from jax.experimental import pallas as pl
from jax.experimental.pallas import tpu as pltpu
from jax.sharding import PartitionSpec as P

MESH = pl.DeviceIdType.MESH
CHUNKS = 4
LAG = 1.5
EARLY = 1.2
RELAY = "none"


def relay_ways(n_row, s, ch):
    if n_row < 4 or s == 0 or RELAY == "none":
        return ()
    if RELAY == "both":
        return (-1, 1)
    return (-1,) if ch % 2 == 0 else (1,)


def kernel(n_col, n_row, rhs, diag, fac, cols, cols_hbm, out, *scratch):
    steps, rows, width = rhs.shape[0], rhs.shape[3], rhs.shape[4]
    slots = fac.shape[4]
    chips = n_col // 2
    half = width // 2
    wide = half // CHUNKS
    fold = max(1, 128 // wide)
    tall = rows // fold
    links = steps - 1
    reach = [sign * h for h in range(n_row - 1, 0, -1) for sign in (-1, 1)]

    (first, away, rv, dv, fv, cp, own, sent, landed, stage,
     f_loc, in_loc, in_send, in_recv, a_send, a_recv, z_send, z_recv, y_send,
     c_send, c_recv, o_loc, o_send, o_recv) = scratch[:24]
    panels = scratch[24:]

    col = lax.axis_index("col")
    row = lax.axis_index("row")
    core = lax.rem(col, 2)
    chip = lax.div(col, 2)
    partner = col + 1 - 2 * core
    mine = pl.ds(pl.multiple_of(core * half, half), half)
    theirs = pl.ds(pl.multiple_of((1 - core) * half, half), half)

    def to(c, r):
        return {"col": c, "row": r}

    def reaches(step):
        return (row + step >= 0) & (row + step < n_row)

    def shifted(d):
        y = lax.rem(lax.div(chip, 2) + lax.div(d, 2), max(1, chips // 2))
        x = lax.rem(lax.rem(chip, 2) + lax.rem(d, 2), 2)
        return y * 2 + x

    barrier = pltpu.get_barrier_semaphore()

    def greet(c, r):
        pl.semaphore_signal(barrier, inc=1, device_id=to(c, r), device_id_type=MESH)

    count = chips
    for step in reach:
        count = count + 2 * reaches(step).astype(jnp.int32)

        @pl.when(reaches(step))
        def _():
            greet(col, row + step)
            greet(partner, row + step)

    for d in range(1, chips):
        greet(shifted(d) * 2 + core, row)
    greet(partner, row)

    start = [
        pltpu.make_async_copy(diag.at[0, 0, 0], dv.at[0, 0], f_loc.at[0]),
        pltpu.make_async_copy(rhs.at[0, 0, 0, :, mine], first.at[0], f_loc.at[1]),
        pltpu.make_async_copy(rhs.at[0, 0, 0, :, theirs], first.at[1], f_loc.at[2]),
    ]
    for c in start:
        c.start()
    later = pl.ds(1, links)
    zero, rest = pl.ds(0, 1), pl.ds(1, links - 1)
    local = {
        "rhs": pltpu.make_async_copy(rhs.at[later, 0, 0, :, mine], rv.at[:, 0], in_loc.at[0]),
        "diag": pltpu.make_async_copy(diag.at[later, 0, 0], dv.at[later, 0], in_loc.at[1]),
        "fac0": pltpu.make_async_copy(fac.at[zero, 0, 0], fv.at[zero, 0], in_loc.at[2]),
        "fac": pltpu.make_async_copy(fac.at[rest, 0, 0], fv.at[rest, 0], in_loc.at[3]),
    }
    for name in ("fac0", "rhs", "diag", "fac"):
        local[name].start()

    def pack(x):
        return x if fold == 1 else jnp.concatenate(
            [x[i * tall:(i + 1) * tall] for i in range(fold)], axis=1)

    def unpack(x):
        return x if fold == 1 else jnp.concatenate(
            [x[:, i * wide:(i + 1) * wide] for i in range(fold)], axis=0)

    def part(ch):
        return pl.ds(ch * wide, wide)

    for c in start:
        c.wait()
    for k in range(2):
        x = jnp.dot(dv[0, 0], first[k], preferred_element_type=jnp.float32).astype(jnp.bfloat16)
        stage[0, k] = x
        for ch in range(CHUNKS):
            piece = pack(x[:, ch * wide:(ch + 1) * wide])
            if k == 0:
                panels[ch][row, 0] = piece
            else:
                away[ch] = piece
    pl.semaphore_wait(barrier, count)

    def remote(src, dst, send, recv, device):
        return pltpu.make_async_remote_copy(
            src_ref=src, dst_ref=dst, send_sem=send, recv_sem=recv,
            device_id=device, device_id_type=MESH)

    def open_copy(ch, k, step):
        way = n_row - 1 + step
        source = panels[ch].at[row, 0] if k == 0 else away.at[ch]
        return remote(source, panels[ch].at[row, k], a_send.at[ch, k, way],
                      a_recv.at[ch, k, row], to(col if k == 0 else partner, row + step))

    def open_wait(ch, k, step):
        remote(panels[ch].at[row + step, k], panels[ch].at[row + step, k], a_send.at[ch, k, 0],
               a_recv.at[ch, k, row + step], to(col, row)).wait_recv()

    for ch in range(CHUNKS):
        for step in reach:
            @pl.when(reaches(step))
            def _():
                for k in range(2):
                    open_copy(ch, k, step).start()
        open_copy(ch, 1, 0).start()

    pair = to(partner, row)
    cross = {
        "cols": remote(cols_hbm, cp, in_send.at[4], in_recv.at[4], pair),
        "fac0": remote(fac.at[zero, 0, 0], fv.at[zero, 1], in_send.at[2], in_recv.at[2], pair),
        "rhs": remote(rhs.at[later, 0, 0, :, theirs], rv.at[:, 1], in_send.at[0], in_recv.at[0], pair),
        "diag": remote(diag.at[later, 0, 0], dv.at[later, 1], in_send.at[1], in_recv.at[1], pair),
        "fac": remote(fac.at[rest, 0, 0], fv.at[rest, 1], in_send.at[3], in_recv.at[3], pair),
    }
    for c in cross.values():
        c.start()

    def arrived(name):
        if name in local:
            local[name].wait()
        cross[name].wait_recv()

    def ways(s, ch):
        return relay_ways(n_row, s, ch)

    def source_of(way):
        return n_row // 2 if way < 0 else n_row // 2 - 1

    def goes(s, ch, step):
        ok = reaches(step)
        for way in ways(s, ch):
            if step == 2 * way:
                ok = ok & (row != source_of(way))
        return ok

    def z_copy(s, ch, step):
        buf = panels[s * CHUNKS + ch]
        return remote(buf.at[row], buf.at[row], z_send.at[s, ch, n_row - 1 + step],
                      z_recv.at[s, ch, row], to(col, row + step))

    def z_wait(s, ch, step):
        buf = panels[s * CHUNKS + ch]
        remote(buf.at[row + step], buf.at[row + step], z_send.at[s, ch, 0],
               z_recv.at[s, ch, row + step], to(col, row)).wait_recv()

    def y_copy(s, ch, way):
        buf, source = panels[s * CHUNKS + ch], source_of(way)
        return remote(buf.at[source], buf.at[source], y_send.at[s, ch],
                      z_recv.at[s, ch, source], to(col, row + way))

    def relay(s, ch):
        for way in ways(s, ch):
            @pl.when(row == source_of(way) + way)
            def _():
                y_copy(s, ch, way).wait_recv()
                y_copy(s, ch, way).start()

    def gathered(s, ch):
        for step in reach[::-1]:
            if s == 0:
                @pl.when(reaches(step))
                def _():
                    for k in range(2):
                        open_wait(ch, k, step)
                continue
            ok = reaches(step)
            for way in ways(s, ch):
                if step == -way:
                    ok = ok & (row != source_of(way) + way)

            @pl.when(ok)
            def _():
                z_wait(s, ch, step)
        if s == 0:
            open_wait(ch, 1, 0)

    def c_copy(s, ch, d):
        return remote(sent.at[s, ch, d - 1], landed.at[s, ch, d - 1], c_send.at[s, ch, d - 1],
                      c_recv.at[s, ch, d - 1], to(shifted(d) * 2 + core, row))

    def out_copies(s, ch):
        begin, size = (ch + 1 - fold) * wide, fold * wide
        span = pl.ds(pl.multiple_of(core * half + begin, size), size)
        src = stage.at[s, :, :, pl.ds(begin, size)]
        keep = pltpu.make_async_copy(src.at[0], out.at[s, 0, 0, :, span], o_loc.at[s, ch])
        give = remote(src.at[1], out.at[s, 0, 0, :, span], o_send.at[s, ch], o_recv.at[s, ch], pair)
        return keep, give

    opened = [
        pltpu.make_async_copy(stage.at[0, 0], out.at[0, 0, 0, :, mine], f_loc.at[1]),
        pltpu.make_async_copy(stage.at[0, 1], out.at[0, 0, 0, :, theirs], f_loc.at[2]),
    ]
    for c in opened:
        c.start()

    def solve(s, ch):
        for d in range(1, chips):
            c_copy(s - 1, ch, d).wait_recv()
        for k in range(2):
            block = dv[s, k]
            right = rv[s - 1, k, :, part(ch)]
            total = own[ch, k]
            for d in range(1, chips):
                total = total + unpack(landed[s - 1, ch, d - 1, k]).astype(jnp.float32)
            rem = right.astype(jnp.float32) - total
            high = rem.astype(jnp.bfloat16)
            low = (rem - high.astype(jnp.float32)).astype(jnp.bfloat16)
            x = jnp.dot(jnp.concatenate([block, block], axis=1),
                        jnp.concatenate([high, low], axis=0),
                        preferred_element_type=jnp.float32).astype(jnp.bfloat16)
            if s < links:
                panels[s * CHUNKS + ch][row, k] = pack(x)
            stage[s, k, :, part(ch)] = x
        if s < links:
            for step in reach:
                @pl.when(goes(s, ch, step))
                def _():
                    z_copy(s, ch, step).start()
        if ch % fold == fold - 1:
            for c in out_copies(s, ch):
                c.start()

    def term(s, ch, other, k):
        buf = panels[s * CHUNKS + ch]
        t = other * 2 + (core if k == 0 else 1 - core)
        left, right = [], []
        for slot, index in ((0, cols), (1, cp)):
            for m in range(slots):
                left.append(fv[s, slot, t, m])
                right.append(unpack(buf[index[s, 0, 0, m, t], slot]))
        return jnp.dot(jnp.concatenate(left, axis=1), jnp.concatenate(right, axis=0),
                       preferred_element_type=jnp.float32)

    def spread(s, ch):
        def one(d):
            other = shifted(d)
            for k in range(2):
                sent[s, ch, d - 1, k] = pack(term(s, ch, other, k).astype(jnp.bfloat16))
            c_copy(s, ch, d).start()

        if chips <= 4:
            for d in range(chips - 1, 0, -1):
                one(d)
        else:
            @pl.loop(1, chips)
            def _(d):
                one(d)
        for k in range(2):
            own[ch, k] = term(s, ch, chip, k)

    items = [(s, ch) for s in range(links) for ch in range(CHUNKS)]
    plan = [(i, 0, i) for i in range(len(items))]
    plan += [(i + LAG, 1, i) for i in range(len(items))]
    plan += [(i - EARLY, 2, i) for i in range(CHUNKS, len(items))]
    for _, what, i in sorted(plan):
        s, ch = items[i]
        if what == 0:
            if i == 0:
                arrived("cols")
                arrived("fac0")
            if i == CHUNKS:
                arrived("fac")
            gathered(s, ch)
            spread(s, ch)
        elif what == 1:
            if i == 0:
                arrived("rhs")
                arrived("diag")
            solve(s + 1, ch)
        else:
            relay(s, ch)

    for c in cross.values():
        c.wait_send()
    for c in opened:
        c.wait()
    for ch in range(CHUNKS):
        for step in reach:
            @pl.when(reaches(step))
            def _():
                for k in range(2):
                    open_copy(ch, k, step).wait_send()
        open_copy(ch, 1, 0).wait_send()
    for s in range(steps):
        for ch in range(CHUNKS):
            if s > 0 and ch % fold == fold - 1:
                keep, give = out_copies(s, ch)
                keep.wait()
                give.wait()
            if 0 < s < links:
                for step in reach:
                    @pl.when(goes(s, ch, step))
                    def _():
                        z_copy(s, ch, step).wait_send()
                for way in ways(s, ch):
                    @pl.when(row == source_of(way) + way)
                    def _():
                        y_copy(s, ch, way).wait_send()
            if s < links:
                for d in range(1, chips):
                    c_copy(s, ch, d).wait_send()


def on_device(n_col, n_row, rhs, diag_inv, factor, columns):
    steps, rows, width = rhs.shape[0], rhs.shape[3], rhs.shape[4]
    columns = jnp.swapaxes(columns, 3, 4)
    targets, slots = factor.shape[3], factor.shape[4]
    chips, half = n_col // 2, width // 2
    wide, links = half // CHUNKS, steps - 1
    fold = max(1, 128 // wide)
    packed = (rows // fold, wide * fold)
    bf16 = jnp.bfloat16
    dma = pltpu.SemaphoreType.DMA
    scratch = [
        pltpu.VMEM((2, rows, half), bf16),
        pltpu.VMEM((CHUNKS,) + packed, bf16),
        pltpu.VMEM((links, 2, rows, half), bf16),
        pltpu.VMEM((steps, 2, rows, rows), bf16),
        pltpu.VMEM((links, 2, targets, slots, rows, rows), bf16),
        pltpu.SMEM(columns.shape, jnp.int32),
        pltpu.VMEM((CHUNKS, 2, rows, wide), jnp.float32),
        pltpu.VMEM((links, CHUNKS, chips - 1, 2) + packed, bf16),
        pltpu.VMEM((links, CHUNKS, chips - 1, 2) + packed, bf16),
        pltpu.VMEM((steps, 2, rows, half), bf16),
        dma((3,)), dma((4,)), dma((5,)), dma((5,)),
        dma((CHUNKS, 2, 2 * n_row - 1)), dma((CHUNKS, 2, n_row)),
        dma((links, CHUNKS, 2 * n_row - 1)), dma((links, CHUNKS, n_row)), dma((links, CHUNKS)),
        dma((links, CHUNKS, chips - 1)), dma((links, CHUNKS, chips - 1)),
        dma((steps, CHUNKS)), dma((steps, CHUNKS)), dma((steps, CHUNKS)),
    ] + [pltpu.VMEM((n_row, 2) + packed, bf16) for _ in range(links * CHUNKS)]
    anywhere = pl.BlockSpec(memory_space=pl.ANY)
    return pl.pallas_call(
        functools.partial(kernel, n_col, n_row),
        out_shape=jax.ShapeDtypeStruct(rhs.shape, bf16),
        in_specs=[anywhere, anywhere, anywhere, pl.BlockSpec(memory_space=pltpu.SMEM), anywhere],
        out_specs=anywhere,
        scratch_shapes=scratch,
        compiler_params=pltpu.CompilerParams(
            collective_id=0, has_side_effects=True, vmem_limit_bytes=60 * 1024 * 1024),
        name="levels",
    )(rhs, diag_inv, factor, columns, columns)


def solution(mesh):
    n_col, n_row = mesh.shape["col"], mesh.shape["row"]
    return jax.shard_map(
        functools.partial(on_device, n_col, n_row),
        mesh=mesh,
        in_specs=(
            P(None, "col", "row", None, None),
            P(None, "col", "row", None, None),
            P(None, "col", "row", None, None, None, None),
            P(None, "col", "row", None, None),
        ),
        out_specs=P(None, "col", "row", None, None),
        check_vma=False,
    )
```

time: 81.6 us -> 77.3 us (0.947)
  Pallas kernels: 79.4 us -> 75 us
    pallas_call x1, Pallas kernels: 79.4 us -> 75 us  [on_device(): pl.pallas_call(functools.partial(kernel, n_col, n_row), out_shape=jax.Sha...]
where the time goes in v1:
time: 77.3 us; the launch traced here: 77.1 us
  Pallas kernels  75 us (97%)
  local copies, waits for them, and re-layouts  2.1 us (3%)
    pallas_call x1, Pallas kernels, on_device(): pl.pallas_call(functools.partial(kernel, n_col, n_row), out_shape=jax.Sha...  75 us
    unnamed x1, local copies, waits for them, and re-layouts  2.1 us

profile of v1, /device:TPU:0, one launch (start us, length us, event | category | flops | bytes accessed | tf_op | source)
XLA Modules:
  0.0 77.1 jit_solution(3547307259402733017)
XLA Ops:
  0.0 75.0 %levels.1 = bf16[6,1,1,128,512]{4,3,2,1,0:T(8,128)(2,1)} custom-call(bf16[6,1,1,128,512]{4,3,2,1,0:T(8,128)(2,1)} %rhs.1, bf16[6,1,1,128,128]{4,3,2,1,0:T(8,128)(2,1)} %diag.1, bf16[5,1,1,8,2,128,128]{6,5,4,3,2,1,0:T(8,128)(2,1)} %fac.1, s32[5,1,1,2,8]{4,3,2,1,0:T(2,128)} %bitcast.1, s32[5,1,1,2,8]{4,3,2,1,0:T(2,128)} %bitcast.2), custom_call_target="tpu_custom_call" | custom-call | tf_op jit(solution)/shard_map/levels/pallas_call | solution.py:368
  75.0 2.1 %copy.6 = bf16[6,1,1,128,512]{4,3,2,1,0:T(8,128)(2,1)} copy(bf16[6,1,1,128,512]{4,3,2,1,0:T(8,128)(2,1)} %levels.1) | data formatting | bytes 1572864
